TPU v7x, 256 devices: a whole 4x4x8 slice. The times are simulated.
256 devices in a mesh: expert: 8 (over x, core), latent: 32 (over y, z).
Axes of the slice: x: 4, y: 4, z: 8, core: 2. Of those that a mesh axis runs over, the one named last changes fastest.
Arguments:
- tokens: bfloat16 [2048, 2560], P(('expert', 'latent')), may hold values from -6 to 6
- route: int32 [2048, 1], P(('expert', 'latent')), may hold values from 0 to 7; in each aligned block of 8 rows (0 to 7, 8 to 15, ...) at most 2 rows name the same one
- blocks: int32 [2048, 64], P(('expert', 'latent')), may hold values from 0 to 255, all different within a row
- weight: bfloat16 [8, 2560, 32768], P('expert', None, 'latent'), may hold values from -0.125 to 0.125
- enc_bias: float32 [8, 32768], P('expert', 'latent'), may hold values from -3 to 3
- dec_bias: float32 [2560], replicated, may hold values from -3 to 3
Outputs:
- grad_weight: bfloat16 [8, 2560, 32768], P('expert', None, 'latent')
- grad_enc: float32 [8, 32768], P('expert', 'latent')
- grad_dec: float32 [2560], replicated
- loss: float32 [], replicated
Inputs may be any that keep to these rules, and one draw needn't show every extreme that they name: `route`: within the rows of one device (aligned blocks of 8 rows) no expert is named by more than 2 rows. Each row lists 64 different blocks.
All inputs are finite; a program needn't handle non-finite values.
Results may differ from a plain program's by a relative error of at most 0.012.
The roundings to bfloat16 on the way count: a program that leaves them out, or rounds other values in their place, can miss the bound.
Values may be sent and summed in bfloat16 or wider, within the bound.
No kernel may reach another device: no remote copies, remote signals or barrier semaphores. Data moves between devices by JAX's collectives and lax.ppermute only.
A program may use at most 128 MiB of HBM per device.

v0:
```python
import jax
import jax.numpy as jnp
from jax import lax
from jax.sharding import PartitionSpec as P

BLK = 128
CAP = 2


def shards(tokens, route, blocks, weight, enc_bias, dec_bias):
    n_expert = lax.axis_size("expert")
    n_latent = lax.axis_size("latent")
    width = tokens.shape[1]
    list_len = blocks.shape[1]
    expert_of = route[:, 0]
    one_hot = (expert_of[:, None] == jnp.arange(n_expert, dtype=jnp.int32)[None, :]).astype(
        jnp.int32
    )
    earlier = jnp.sum((jnp.cumsum(one_hot, axis=0) - one_hot) * one_hot, axis=1)
    target = expert_of * CAP + earlier
    send_rows = jnp.zeros((n_expert * CAP, width), jnp.bfloat16).at[target].set(tokens)
    send_rows = send_rows.reshape(n_expert, CAP, width)
    send_lists = jnp.full((n_expert * CAP, list_len), -1, jnp.int32).at[target].set(blocks)
    send_lists = send_lists.reshape(n_expert, CAP, list_len)
    got_rows, got_lists = (
        lax.all_to_all(send_rows, "expert", split_axis=0, concat_axis=0, tiled=True),
        lax.all_to_all(send_lists, "expert", split_axis=0, concat_axis=0, tiled=True),
    )
    all_rows, all_lists = (
        lax.all_gather(got_rows[None], "latent", axis=0, tiled=True),
        lax.all_gather(got_lists[None], "latent", axis=0, tiled=True),
    )
    token_rows = all_rows.reshape(-1, width)
    listed = all_lists.reshape(-1, list_len)
    row_count = token_rows.shape[0]
    valid = (listed[:, 0] >= 0).astype(jnp.float32)
    slice_index = lax.axis_index("latent")
    weights_here = weight[0]
    per_slice = weights_here.shape[1] // BLK
    own_blocks = slice_index * per_slice + jnp.arange(per_slice, dtype=jnp.int32)
    chosen = jnp.any(listed[:, :, None] == own_blocks[None, None, :], axis=1).astype(jnp.float32)
    mask = jnp.repeat(chosen, BLK, axis=1)
    rows_f32 = token_rows.astype(jnp.float32)
    shifted = (rows_f32 - dec_bias).astype(jnp.bfloat16)
    pre_act = jnp.dot(shifted, weights_here, preferred_element_type=jnp.float32) + enc_bias[0]
    active = jnp.maximum(pre_act, 0.0) * mask
    active_bf = active.astype(jnp.bfloat16)
    share = row_count // n_latent
    first_row = slice_index * share
    along_width = (((1,), (1,)), ((), ()))
    partial_sum = lax.dot_general(
        active_bf, weights_here, along_width, preferred_element_type=jnp.float32
    )
    summed = lax.psum(partial_sum, "latent")
    error_all = (summed + dec_bias - rows_f32) * valid[:, None]
    error_bf = error_all.astype(jnp.bfloat16)
    error_share = lax.dynamic_slice_in_dim(error_all, first_row, share, 0)
    grad_act = jnp.dot(error_bf, weights_here, preferred_element_type=jnp.float32)
    grad_pre = grad_act * (pre_act > 0.0).astype(jnp.float32) * mask
    grad_pre_bf = grad_pre.astype(jnp.bfloat16)
    along_rows = (((0,), (0,)), ((), ()))
    grad_here = lax.dot_general(
        shifted, grad_pre_bf, along_rows, preferred_element_type=jnp.float32
    )
    grad_here = grad_here + lax.dot_general(
        error_bf, active_bf, along_rows, preferred_element_type=jnp.float32
    )
    grad_bias = jnp.sum(grad_pre, axis=0)
    pulled = jnp.dot(
        weights_here, grad_bias.astype(jnp.bfloat16), preferred_element_type=jnp.float32
    )
    bias_term = jnp.sum(error_share, axis=0) - pulled
    loss_term = 0.5 * jnp.sum(error_share * error_share)
    grad_dec, loss_sum = lax.psum((bias_term, loss_term), ("expert", "latent"))
    loss = loss_sum / (tokens.shape[0] * n_expert * n_latent)
    return (grad_here.astype(jnp.bfloat16)[None], grad_bias[None], grad_dec, loss)


def solution(mesh):
    return jax.shard_map(
        shards,
        mesh=mesh,
        in_specs=(
            P(("expert", "latent"), None),
            P(("expert", "latent"), None),
            P(("expert", "latent"), None),
            P("expert", None, "latent"),
            P("expert", "latent"),
            P(),
        ),
        out_specs=(P("expert", None, "latent"), P("expert", "latent"), P(), P()),
        check_vma=False,
    )
```

profile of v0, /device:TPU:1, one launch (start us, length us, event | category | flops | bytes accessed | tf_op | source)
XLA Modules:
  0.0 402.3 jit_solution(3232776257881222928)
XLA Ops:
  7.2 0.0 all-gather.4.cloned.1.call-start
  7.2 0.7 fusion.24
  8.0 0.8 select_reduce_fusion
  8.8 0.7 fusion.25
  9.5 0.9 scatter_custom_fusion
  10.4 11.2 %all_to_all.10 = bf16[8,2,2560]{2,1,0:T(2,128)(2,1)} all-to-all(bf16[8,2,2560]{2,1,0:T(2,128)(2,1)S(1)} %reshape.33), channel_id=1, replica_groups=mesh['expert'=8,'latent'=32] {'expert'}, dimensions={0} | all-to-all | bytes 163840 | tf_op jit(solution)/shard_map/all_to_all | solution.py:26
  21.6 0.0 all-gather.4.cloned.1.call-update
  21.7 0.8 scatter_custom_fusion.1
  22.4 0.7 reshape.68
  23.1 4.0 all-to-all-start.1
  27.1 4.5 %all-to-all-done.1 = s32[8,1,128]{2,1,0:T(1,128)S(1)} async-done(((s32[8,1,128]{2,1,0:T(1,128)}), s32[8,1,128]{2,1,0:T(1,128)S(1)}, u32[]{:S(2)}, u32[]{:S(2)}) %all-to-all-start.1) | async-done | bytes 4128 | tf_op jit(solution)/shard_map/all_to_all | solution.py:27
  31.6 0.5 broadcast.43
  32.2 0.7 reduce.4
  32.8 0.1 reshape.69
  32.9 40.8 %all-gather.1 = s32[256,2,64]{2,1,0:T(2,128)S(1)} all-gather(s32[8,2,64]{2,1,0:T(2,128)S(1)} %reshape.69), channel_id=3, replica_groups=mesh['expert'=8,'latent'=32] {'latent'}, dimensions={0}, use_global_device_ids=true | all-gather | bytes 135168 | tf_op jit(solution)/shard_map/all_gather | solution.py:31
  73.7 0.1 copy.12
  73.8 0.2 compare_reduce_fusion
  74.1 0.1 copy.13
  74.2 24.0 %all-gather.4.cloned.1.call-done = bf16[256,2,2560]{2,1,0:T(2,128)(2,1)} async-done(((bf16[8,2,2560]{2,1,0:T(2,128)(2,1)}), bf16[256,2,2560]{2,1,0:T(2,128)(2,1)}) %all-gather.4.cloned.1.call-update) | async-done | bytes 2621456 | tf_op jit(solution)/shard_map/all_gather | solution.py:30
  98.1 3.5 convert_element_type.56
  101.7 2.3 subtract_convert_fusion
  104.0 0.0 copy-start.6
  104.0 2.6 convert_element_type.47
  106.6 0.6 broadcast_in_dim.32
  107.2 0.0 copy-start.1
  107.2 0.0 copy-done.6
  107.2 0.0 slice-start.3
  107.3 8.7 %fusion.11 = (bf16[512,1024]{1,0:T(8,128)(2,1)S(1)}, f32[512,1024]{1,0:T(8,128)}) fusion(f32[64,8,8,128]{3,2,1,0:T(8,128)S(1)} %bitcast.51, f32[1024]{0:T(1024)S(1)} %bitcast.57, bf16[512,2560]{1,0:T(8,128)(2,1)} %convert_element_type.47, bf16[1,2560,1024]{2,1,0:T(8,128)(2,1)} %param.9), kind=kOutput, calls=%fused_computation.19 | convolution fusion | flops 2686451712 | bytes 13111296 | tf_op jit(solution)/shard_map/dot_general | solution.py:45
  116.0 1.0 copy-done.3
  117.0 4.7 %fusion.4 = f32[512,2560]{1,0:T(8,128)} fusion(bf16[512,1024]{1,0:T(8,128)(2,1)S(1)} %get-tuple-element.8, bf16[1,2560,1024]{2,1,0:T(8,128)(2,1)S(1)} %bitcast.46), kind=kOutput, calls=%fused_computation.7 | convolution fusion | flops 2684354560 | bytes 11534336 | tf_op jit(solution)/shard_map/dot_general | solution.py:51
  121.7 0.0 all-reduce.3.cloned.1.call-update
  121.7 0.1 convert_reduce_fusion
  121.8 1.6 copy-done
  123.4 2.9 reshape.36
  126.4 168.2 %all-reduce.3.cloned.1.call-done = f32[512,2560]{1,0:T(8,128)} async-done(((f32[512,2560]{1,0:T(8,128)}), f32[512,2560]{1,0:T(8,128)}) %all-reduce.3.cloned.1.call-update) | async-done | bytes 5242896 | tf_op jit(solution)/shard_map/psum | solution.py:54
  294.5 4.9 %subtract_multiply_fusion = f32[512,2560]{1,0:T(8,128)S(1)} fusion(f32[512,2560]{1,0:T(8,128)} %reshape.36, f32[512,2560]{1,0:T(8,128)} %all-reduce.3.cloned.1.call-done, f32[512]{0:T(512)S(1)} %convert_reduce_fusion, f32[2560]{0:T(1024)S(1)} %copy-done.4), kind=kLoop, calls=%fused_computation.11 | loop fusion | flops 3932160 | bytes 15740928 | tf_op jit(solution)/shard_map/mul | solution.py:55
  299.5 0.0 slice-start.1
  299.5 5.9 %fusion.26 = (f32[1024]{0:T(1024)S(1)}, bf16[512,1024]{1,0:T(8,128)(2,1)S(1)}) fusion(f32[64,8,8,128]{3,2,1,0:T(8,128)S(1)} %bitcast.52, bf16[1,2560,1024]{2,1,0:T(8,128)(2,1)} %param.9, f32[512,2560]{1,0:T(8,128)S(1)} %subtract_multiply_fusion, f32[512,1024]{1,0:T(8,128)S(1)} %copy-done.7, f32[1024]{0:T(1024)S(1)} %bitcast.58), kind=kOutput, calls=%fused_computation.40 | convolution fusion | flops 2688809984 | bytes 15736832 | tf_op jit(solution)/shard_map/dot_general | solution.py:58
  305.4 0.0 copy-start.5
  305.4 0.0 slice-done
  305.4 0.0 slice-done.1
  305.4 0.0 slice-start.4
  305.5 3.0 fusion.9
  308.5 0.0 slice-start.5
  308.5 6.5 %fusion.8 = bf16[1,2560,1024]{2,1,0:T(8,128)(2,1)} fusion(f32[2560,1024]{1,0:T(8,128)S(1)} %fusion.9, bf16[512,1024]{1,0:T(8,128)(2,1)} %copy-done.3, f32[512,2560]{1,0:T(8,128)S(1)} %subtract_multiply_fusion), kind=kOutput, calls=%fused_computation.14 | convolution fusion | flops 2690908160 | bytes 22020096 | tf_op jit(solution)/shard_map/dot_general | solution.py:65
  315.0 0.6 multiply_reduce_fusion
  315.6 1.5 fusion.16
  317.8 75.9 %all-reduce = (f32[2560]{0:T(1024)}, f32[]{:T(128)}) all-reduce(f32[2560]{0:T(1024)S(1)} %sub.28, f32[]{:T(128)S(6)} %mul_shard_map.3), channel_id=1, replica_groups=mesh['expert'=8,'latent'=32] {'expert','latent'}, use_global_device_ids=true, to_apply=%region_8.9 | all-reduce | flops 2561 | bytes 20488 | tf_op jit(solution)/shard_map/psum | solution.py:74
  (27 shorter events, 0.1 us)
Async XLA Ops:
  7.2 94.5 %copy-start.4 = (f32[2560]{0:T(1024)S(1)}, f32[2560]{0:T(1024)}, u32[]{:S(2)}) copy-start(f32[2560]{0:T(1024)} %param.11) | copy-start | bytes 30724
  7.2 91.0 %all-gather.4.cloned.1.call-start = ((), (), s32[]{:S(2)}) async-start(), calls=%async_computation.3 | async-start | bytes 2703360 | tf_op jit(solution)/shard_map/all_gather | solution.py:30
  23.1 8.5 %all-to-all-start.1 = ((s32[8,1,128]{2,1,0:T(1,128)}), s32[8,1,128]{2,1,0:T(1,128)S(1)}, u32[]{:S(2)}, u32[]{:S(2)}) async-start(s32[8,1,128]{2,1,0:T(1,128)} %reshape.68), calls=%async_computation.1 | async-start | bytes 8192 | tf_op jit(solution)/shard_map/all_to_all | solution.py:27
  27.1 267.4 %all-reduce.3.cloned.1.call-start = ((), (), s32[]{:S(2)}) async-start(), calls=%async_computation.2 | async-start | bytes 10485760 | tf_op jit(solution)/shard_map/psum | solution.py:54
  104.0 3.2 copy-start.6
  106.6 10.4 %slice-start.2 = ((s8[5242880]{0:T(1024)(128)(4,1)}), s8[4194304]{0:T(1024)(128)(4,1)S(1)}, s32[]{:S(2)}) async-start(s8[5242880]{0:T(1024)(128)(4,1)} %bitcast.45), calls=%async_computation.6 | async-start | bytes 8388608
  107.2 8.8 %copy-start.1 = (f32[512,8,128]{2,1,0:T(8,128)}, f32[512,8,128]{2,1,0:T(8,128)S(1)}, u32[]{:S(2)}) copy-start(f32[512,8,128]{2,1,0:T(8,128)S(1)} %broadcast_in_dim.32) | copy-start | bytes 6291460
  107.2 9.7 %slice-start.3 = ((s8[5242880]{0:T(1024)(128)(4,1)}), s8[1048576]{0:T(1024)(128)(4,1)S(1)}, s32[]{:S(2)}) async-start(s8[5242880]{0:T(1024)(128)(4,1)} %bitcast.45), calls=%async_computation.7 | async-start | bytes 2097152
  116.0 1.0 copy-start.3
  121.7 1.7 copy-start
  126.3 173.1 %copy-start.2 = (f32[512,8,128]{2,1,0:T(8,128)S(1)}, f32[512,8,128]{2,1,0:T(8,128)}, u32[]{:S(2)}) copy-start(f32[512,8,128]{2,1,0:T(8,128)} %copy-done.1) | copy-start | bytes 6291460
  294.5 4.9 %copy-start.7 = (f32[512,1024]{1,0:T(8,128)S(1)}, f32[512,1024]{1,0:T(8,128)}, u32[]{:S(2)}) copy-start(f32[512,1024]{1,0:T(8,128)} %get-tuple-element.9) | copy-start | bytes 6291460
  294.5 10.9 %slice-start = ((s8[5242880]{0:T(1024)(128)(4,1)}), s8[1048576]{0:T(1024)(128)(4,1)S(1)}, s32[]{:S(2)}) async-start(s8[5242880]{0:T(1024)(128)(4,1)} %bitcast.42), calls=%async_computation.4 | async-start | bytes 2097152
  299.5 6.0 %slice-start.1 = ((s8[5242880]{0:T(1024)(128)(4,1)}), s8[4194304]{0:T(1024)(128)(4,1)S(1)}, s32[]{:S(2)}) async-start(s8[5242880]{0:T(1024)(128)(4,1)} %bitcast.42), calls=%async_computation.5 | async-start | bytes 8388608
  305.4 10.2 %copy-start.5 = (f32[1024]{0:T(1024)}, f32[1024]{0:T(1024)S(1)}, u32[]{:S(2)}) copy-start(f32[1024]{0:T(1024)S(1)} %get-tuple-element.10) | copy-start | bytes 12292
  305.4 10.2 %slice-start.4 = ((s8[5242880]{0:T(1024)(128)(4,1)}), s8[4194304]{0:T(1024)(128)(4,1)S(1)}, s32[]{:S(2)}) async-start(s8[5242880]{0:T(1024)(128)(4,1)} %bitcast.47), calls=%async_computation.8 | async-start | bytes 8388608
  308.5 7.2 %slice-start.5 = ((s8[5242880]{0:T(1024)(128)(4,1)}), s8[1048576]{0:T(1024)(128)(4,1)S(1)}, s32[]{:S(2)}) async-start(s8[5242880]{0:T(1024)(128)(4,1)} %bitcast.47), calls=%async_computation.9 | async-start | bytes 2097152
Sparse Core Ops, SparseCore 0:
  21.8 76.3 all-gather.3
  121.8 172.6 all-reduce.2
where the time goes:
time: 403 us; the launch traced here: 402 us
  waiting for transfers between devices  197 us (49%)
  blocking collectives  128 us (32%)
  matrix products  30.3 us (8%)
  between operations  16.7 us (4%)
  other arithmetic  14.6 us (4%)
  local copies, waits for them, and re-layouts  12 us (3%)
  starting transfers between devices  4.05 us (1%)
    psum x1, waiting for transfers between devices, shards(): summed = lax.psum(partial_sum, 'latent')  168 us
    psum x1, blocking collectives, shards(): grad_dec, loss_sum = lax.psum((bias_term, loss_term), ('expert', 'latent'))  75.9 us
    all_gather x1, blocking collectives, shards(): lax.all_gather(got_lists[None], 'latent', axis=0, tiled=True)  40.8 us
    all_gather x1, waiting for transfers between devices, shards(): lax.all_gather(got_rows[None], 'latent', axis=0, tiled=True)  24 us
    all_to_all x1, blocking collectives, shards(): lax.all_to_all(send_rows, 'expert', split_axis=0, concat_axis=0, tiled=True)  11.2 us
    dot_general x1, matrix products, shards(): jnp.dot(shifted, weights_here, preferred_element_type=jnp.float32)  8.73 us
  transfers between devices with their start and end apart: 3, of which 3 were waited for; matrix products, arithmetic and copies ran while one was open for 2% of the time, Pallas kernels for 0%

commit v1 on v0

--- a/solution.py
+++ b/solution.py
@@ -71,7 +71,7 @@
     )
     bias_term = jnp.sum(error_share, axis=0) - pulled
     loss_term = 0.5 * jnp.sum(error_share * error_share)
-    grad_dec, loss_sum = lax.psum((bias_term, loss_term), ("expert", "latent"))
+    grad_dec, loss_sum = lax.psum(lax.psum((bias_term, loss_term), "expert"), "latent")
     loss = loss_sum / (tokens.shape[0] * n_expert * n_latent)
     return (grad_here.astype(jnp.bfloat16)[None], grad_bias[None], grad_dec, loss)
 

time: 403 us -> 491 us (1.22)
  the two profiles are of different devices: /device:TPU:1 before, /device:TPU:0 now
where the time goes in v1:
time: 491 us
  blocking collectives  227 us (46%)
  waiting for transfers between devices  186 us (38%)
  matrix products  30.3 us (6%)
  between operations  16.7 us (3%)
  other arithmetic  14.6 us (3%)
  local copies, waits for them, and re-layouts  12 us (2%)
    psum x1, waiting for transfers between devices, shards(): summed = lax.psum(partial_sum, 'latent')  165 us
    psum x1, blocking collectives, shards(): lax.psum(lax.psum((bias_term, loss_term), 'expert'), 'latent')  141 us
    all_gather x1, blocking collectives, shards(): lax.all_gather(got_lists[None], 'latent', axis=0, tiled=True)  52 us
    psum x1, blocking collectives, shards(): lax.psum((bias_term, loss_term), 'expert')  25.8 us
    all_gather x1, waiting for transfers between devices, shards(): lax.all_gather(got_rows[None], 'latent', axis=0, tiled=True)  16.2 us
  transfers between devices with their start and end apart: 3, of which 3 were waited for; matrix products, arithmetic and copies ran while one was open for 1% of the time, Pallas kernels for 0%

profile of v1, /device:TPU:0, one launch (start us, length us, event | category | flops | bytes accessed | tf_op | source)
XLA Modules:
  0.0 490.8 jit_solution(9798718834703232826)
XLA Ops:
  7.2 0.0 all-gather.4.cloned.1.call-start
  7.2 0.7 fusion.24
  8.0 0.8 select_reduce_fusion
  8.8 0.7 fusion.25
  9.5 0.9 scatter_custom_fusion
  10.4 8.8 %all_to_all.10 = bf16[8,2,2560]{2,1,0:T(2,128)(2,1)} all-to-all(bf16[8,2,2560]{2,1,0:T(2,128)(2,1)S(1)} %reshape.33), channel_id=1, replica_groups=mesh['expert'=8,'latent'=32] {'expert'}, dimensions={0} | all-to-all | bytes 163840 | tf_op jit(solution)/shard_map/all_to_all | solution.py:26
  19.2 0.0 all-gather.4.cloned.1.call-update
  19.2 0.8 scatter_custom_fusion.1
  20.0 0.7 reshape.68
  20.7 3.3 all-to-all-start.1
  24.0 0.0 all-reduce.4.cloned.1.call-start
  24.1 5.0 %all-to-all-done.1 = s32[8,1,128]{2,1,0:T(1,128)S(1)} async-done(((s32[8,1,128]{2,1,0:T(1,128)}), s32[8,1,128]{2,1,0:T(1,128)S(1)}, u32[]{:S(2)}, u32[]{:S(2)}) %all-to-all-start.1) | async-done | bytes 4128 | tf_op jit(solution)/shard_map/all_to_all | solution.py:27
  29.1 0.5 broadcast.43
  29.6 0.7 reduce.4
  30.3 0.1 reshape.69
  30.4 52.0 %all-gather.1 = s32[256,2,64]{2,1,0:T(2,128)S(1)} all-gather(s32[8,2,64]{2,1,0:T(2,128)S(1)} %reshape.69), channel_id=3, replica_groups=mesh['expert'=8,'latent'=32] {'latent'}, dimensions={0}, use_global_device_ids=true | all-gather | bytes 135168 | tf_op jit(solution)/shard_map/all_gather | solution.py:31
  82.3 0.1 copy.12
  82.4 0.2 compare_reduce_fusion
  82.7 0.1 copy.13
  82.8 16.2 %all-gather.4.cloned.1.call-done = bf16[256,2,2560]{2,1,0:T(2,128)(2,1)} async-done(((bf16[8,2,2560]{2,1,0:T(2,128)(2,1)}), bf16[256,2,2560]{2,1,0:T(2,128)(2,1)}) %all-gather.4.cloned.1.call-update) | async-done | bytes 2621456 | tf_op jit(solution)/shard_map/all_gather | solution.py:30
  99.0 3.5 convert_element_type.56
  102.5 2.3 subtract_convert_fusion
  104.8 0.0 copy-start.6
  104.8 2.6 convert_element_type.47
  107.5 0.6 broadcast_in_dim.32
  108.1 0.0 slice-start.3
  108.1 8.7 %fusion.11 = (bf16[512,1024]{1,0:T(8,128)(2,1)S(1)}, f32[512,1024]{1,0:T(8,128)}) fusion(f32[64,8,8,128]{3,2,1,0:T(8,128)S(1)} %bitcast.51, f32[1024]{0:T(1024)S(1)} %bitcast.57, bf16[512,2560]{1,0:T(8,128)(2,1)} %convert_element_type.47, bf16[1,2560,1024]{2,1,0:T(8,128)(2,1)} %param.9), kind=kOutput, calls=%fused_computation.19 | convolution fusion | flops 2686451712 | bytes 13111296 | tf_op jit(solution)/shard_map/dot_general | solution.py:45
  116.8 1.0 copy-done.3
  117.8 4.7 fusion.4
  122.5 0.0 all-reduce.4.cloned.1.call-update
  122.6 0.1 convert_reduce_fusion
  122.7 1.6 copy-done
  124.3 2.9 reshape.36
  127.2 165.0 %all-reduce.4.cloned.1.call-done = f32[512,2560]{1,0:T(8,128)} async-done(((f32[512,2560]{1,0:T(8,128)}), f32[512,2560]{1,0:T(8,128)}) %all-reduce.4.cloned.1.call-update) | async-done | bytes 5242896 | tf_op jit(solution)/shard_map/psum | solution.py:54
  292.2 4.9 subtract_multiply_fusion
  297.2 0.0 copy-done.2
  297.2 0.0 copy-done.7
  297.2 0.0 slice-start.1
  297.2 5.9 %fusion.26 = (f32[1024]{0:T(1024)S(1)}, bf16[512,1024]{1,0:T(8,128)(2,1)S(1)}) fusion(f32[64,8,8,128]{3,2,1,0:T(8,128)S(1)} %bitcast.52, bf16[1,2560,1024]{2,1,0:T(8,128)(2,1)} %param.9, f32[512,2560]{1,0:T(8,128)S(1)} %subtract_multiply_fusion, f32[512,1024]{1,0:T(8,128)S(1)} %copy-done.7, f32[1024]{0:T(1024)S(1)} %bitcast.58), kind=kOutput, calls=%fused_computation.40 | convolution fusion | flops 2688809984 | bytes 15736832 | tf_op jit(solution)/shard_map/dot_general | solution.py:58
  303.1 0.0 copy-start.5
  303.2 0.0 slice-start.4
  303.2 3.0 fusion.9
  306.2 0.0 slice-start.5
  306.2 6.5 %fusion.8 = bf16[1,2560,1024]{2,1,0:T(8,128)(2,1)} fusion(f32[2560,1024]{1,0:T(8,128)S(1)} %fusion.9, bf16[512,1024]{1,0:T(8,128)(2,1)} %copy-done.3, f32[512,2560]{1,0:T(8,128)S(1)} %subtract_multiply_fusion), kind=kOutput, calls=%fused_computation.14 | convolution fusion | flops 2690908160 | bytes 22020096 | tf_op jit(solution)/shard_map/dot_general | solution.py:65
  312.7 0.6 multiply_reduce_fusion
  313.3 1.5 fusion.16
  315.5 25.8 %all-reduce.1 = (f32[2560]{0:T(1024)S(1)}, f32[]{:T(128)}) all-reduce(f32[2560]{0:T(1024)S(1)} %sub.28, f32[]{:T(128)S(6)} %mul_shard_map.3), channel_id=1, replica_groups=mesh['expert'=8,'latent'=32] {'expert'}, use_global_device_ids=true, to_apply=%region_8.9 | all-reduce | flops 2561 | bytes 20488 | tf_op jit(solution)/shard_map/psum | solution.py:74
  341.3 140.9 %all-reduce = (f32[2560]{0:T(1024)}, f32[]{:T(128)}) all-reduce(f32[2560]{0:T(1024)S(1)} %get-tuple-element.8, f32[]{:T(128)} %get-tuple-element.9), channel_id=1, replica_groups=mesh['expert'=8,'latent'=32] {'latent'}, use_global_device_ids=true, to_apply=%region_9.10 | all-reduce | flops 2561 | bytes 20488 | tf_op jit(solution)/shard_map/psum | solution.py:74
  (28 shorter events, 0.1 us)
Async XLA Ops:
  7.2 95.4 %copy-start.4 = (f32[2560]{0:T(1024)S(1)}, f32[2560]{0:T(1024)}, u32[]{:S(2)}) copy-start(f32[2560]{0:T(1024)} %param.11) | copy-start | bytes 30724
  7.2 91.8 %all-gather.4.cloned.1.call-start = ((), (), s32[]{:S(2)}) async-start(), calls=%async_computation.3 | async-start | bytes 2703360 | tf_op jit(solution)/shard_map/all_gather | solution.py:30
  20.7 8.4 %all-to-all-start.1 = ((s32[8,1,128]{2,1,0:T(1,128)}), s32[8,1,128]{2,1,0:T(1,128)S(1)}, u32[]{:S(2)}, u32[]{:S(2)}) async-start(s32[8,1,128]{2,1,0:T(1,128)} %reshape.68), calls=%async_computation.1 | async-start | bytes 8192 | tf_op jit(solution)/shard_map/all_to_all | solution.py:27
  24.0 268.2 %all-reduce.4.cloned.1.call-start = ((), (), s32[]{:S(2)}) async-start(), calls=%async_computation.2 | async-start | bytes 10485760 | tf_op jit(solution)/shard_map/psum | solution.py:54
  104.8 3.2 copy-start.6
  107.5 10.4 %slice-start.2 = ((s8[5242880]{0:T(1024)(128)(4,1)}), s8[4194304]{0:T(1024)(128)(4,1)S(1)}, s32[]{:S(2)}) async-start(s8[5242880]{0:T(1024)(128)(4,1)} %bitcast.45), calls=%async_computation.6 | async-start | bytes 8388608
  108.1 8.8 %copy-start.1 = (f32[512,8,128]{2,1,0:T(8,128)}, f32[512,8,128]{2,1,0:T(8,128)S(1)}, u32[]{:S(2)}) copy-start(f32[512,8,128]{2,1,0:T(8,128)S(1)} %broadcast_in_dim.32) | copy-start | bytes 6291460
  108.1 9.7 %slice-start.3 = ((s8[5242880]{0:T(1024)(128)(4,1)}), s8[1048576]{0:T(1024)(128)(4,1)S(1)}, s32[]{:S(2)}) async-start(s8[5242880]{0:T(1024)(128)(4,1)} %bitcast.45), calls=%async_computation.7 | async-start | bytes 2097152
  116.8 1.0 copy-start.3
  122.5 1.7 copy-start
  127.2 170.0 %copy-start.2 = (f32[512,8,128]{2,1,0:T(8,128)S(1)}, f32[512,8,128]{2,1,0:T(8,128)}, u32[]{:S(2)}) copy-start(f32[512,8,128]{2,1,0:T(8,128)} %copy-done.1) | copy-start | bytes 6291460
  292.2 4.9 %copy-start.7 = (f32[512,1024]{1,0:T(8,128)S(1)}, f32[512,1024]{1,0:T(8,128)}, u32[]{:S(2)}) copy-start(f32[512,1024]{1,0:T(8,128)} %get-tuple-element.11) | copy-start | bytes 6291460
  292.2 10.9 %slice-start = ((s8[5242880]{0:T(1024)(128)(4,1)}), s8[1048576]{0:T(1024)(128)(4,1)S(1)}, s32[]{:S(2)}) async-start(s8[5242880]{0:T(1024)(128)(4,1)} %bitcast.42), calls=%async_computation.4 | async-start | bytes 2097152
  297.2 6.0 %slice-start.1 = ((s8[5242880]{0:T(1024)(128)(4,1)}), s8[4194304]{0:T(1024)(128)(4,1)S(1)}, s32[]{:S(2)}) async-start(s8[5242880]{0:T(1024)(128)(4,1)} %bitcast.42), calls=%async_computation.5 | async-start | bytes 8388608
  303.1 10.2 %copy-start.5 = (f32[1024]{0:T(1024)}, f32[1024]{0:T(1024)S(1)}, u32[]{:S(2)}) copy-start(f32[1024]{0:T(1024)S(1)} %get-tuple-element.12) | copy-start | bytes 12292
  303.2 10.2 %slice-start.4 = ((s8[5242880]{0:T(1024)(128)(4,1)}), s8[4194304]{0:T(1024)(128)(4,1)S(1)}, s32[]{:S(2)}) async-start(s8[5242880]{0:T(1024)(128)(4,1)} %bitcast.47), calls=%async_computation.8 | async-start | bytes 8388608
  306.2 7.2 %slice-start.5 = ((s8[5242880]{0:T(1024)(128)(4,1)}), s8[1048576]{0:T(1024)(128)(4,1)S(1)}, s32[]{:S(2)}) async-start(s8[5242880]{0:T(1024)(128)(4,1)} %bitcast.47), calls=%async_computation.9 | async-start | bytes 2097152
Sparse Core Ops, SparseCore 0:
  19.4 79.5 all-gather.3
  122.7 169.5 all-reduce.3
